TPU v7x, 32 devices: a whole 2x2x4 slice. The times are simulated.
32 devices in a mesh: row: 8 (over y, x, core), col: 4 (over z).
Axes of the slice: x: 2, y: 2, z: 4, core: 2. Of those that a mesh axis runs over, the one named last changes fastest.
Arguments:
- fast_pos: float32 [3, 4096], P(None, ('row', 'col')), may hold values from 0 to 1
- fast_vel: float32 [3, 4096], P(None, ('row', 'col')), may hold values from -5 to 5
- fast_charge: float32 [4096], replicated, may hold values from -4 to 4
- fast_owner: int32 [4096], replicated, may hold values from 0 to 1023, as said below
- exclusions: int32 [4096, 4], replicated, may hold values from 0 to 4095, as said below
- slow_pos: float32 [3, 32, 32, 128], P(None, 'row', 'col'), may hold values from 0 to 1
- slow_vel: float32 [3, 32, 32, 128], P(None, 'row', 'col'), may hold values from -5 to 5
- slow_charge: float32 [32, 32, 128], P('row', 'col'), may hold values from -4 to 4
- neighbours: int32 [32, 32, 5], P('row', 'col'), may hold values from 0 to 24, all different within a row
Outputs:
- fast_pos_out: float32 [3, 4096], P(None, ('row', 'col'))
- fast_vel_out: float32 [3, 4096], P(None, ('row', 'col'))
- slow_pos_out: float32 [3, 32, 32, 128], P(None, 'row', 'col')
- slow_vel_out: float32 [3, 32, 32, 128], P(None, 'row', 'col')
Inputs may be any that keep to these rules, and one draw needn't show every extreme that they name: `fast_owner`: atoms a and b with a % (256) == b % (256) share an owner. `exclusions`: the partners of atom a are atoms b != a with b % (256) == a % 256; a partner may repeat. `neighbours`: the entries of one cell are distinct.
All inputs are finite; a program needn't handle non-finite values.
Results may differ from a plain program's by a relative error of at most 0.0003.
Values sent between devices are 32-bit elements; how exact they have to be, the bound alone decides.
No kernel may reach another device: no remote copies, remote signals or barrier semaphores. Data moves between devices by JAX's collectives and lax.ppermute only.
A program may use at most 64 MiB of HBM per device.

v0:
```python
import jax
import jax.numpy as jnp
from jax import lax
from jax.sharding import PartitionSpec as P

FAST = 4096
CELL = 128
INNER = 4
fast_coupling = 1.0
slow_coupling = 0.1
outer_dt = 0.2


def with_halo(x, sides, width):
    for axis, dim in sides:
        count, length = (lax.axis_size(axis), x.shape[dim])
        up = [(i, (i + 1) % count) for i in range(count)]
        down = [(j, i) for i, j in up]
        last = lax.slice_in_dim(x, length - width, length, axis=dim)
        initial = lax.slice_in_dim(x, 0, width, axis=dim)
        before = lax.ppermute(last, axis, up)
        after = lax.ppermute(initial, axis, down)
        x = jnp.concatenate([before, x, after], axis=dim)
    return x


def owner_coords(owner, total_cols):
    grid_row = (owner // total_cols).astype(jnp.float32)
    grid_col = (owner % total_cols).astype(jnp.float32)
    return jnp.stack([grid_row, grid_col, jnp.zeros_like(grid_row)])


def pair_fast(pos_a, cell_a, charge_a, exclude_a, pos_b, cell_b, charge_b, index_b):
    delta = pos_a[:, :, None] - pos_b[:, None, :] + (cell_a[:, :, None] - cell_b[:, None, :])
    dist_sq = jnp.sum(delta * delta, axis=0) + 1.0
    inverse = 1.0 / (dist_sq * jnp.sqrt(dist_sq))
    barred = jnp.any(exclude_a[:, :, None] == index_b[None, None, :], axis=1)
    weight = jnp.where(barred, jnp.float32(0.0), charge_a[:, None] * charge_b[None, :] * inverse)
    return fast_coupling * jnp.sum(weight[None] * delta, axis=2)


def slow_cells(own, views, lists):
    force = jnp.zeros((3,) + own.shape[1:], jnp.float32)
    offsets = jnp.arange(25, dtype=jnp.int32)
    for slot in range(lists.shape[-1]):
        chosen = lists[..., slot]
        pick = (chosen[..., None] == offsets).astype(jnp.float32)
        other = jnp.einsum("abo,oxabn->xabn", pick, views, precision=lax.Precision.HIGHEST)
        shift_row = (chosen // 5 - 2).astype(jnp.float32)
        shift_col = (chosen % 5 - 2).astype(jnp.float32)
        shift = jnp.stack([shift_row, shift_col, jnp.zeros_like(shift_row)])
        delta = own[0:3, :, :, :, None] - (other[0:3, :, :, None, :] + shift[:, :, :, None, None])
        dist_sq = jnp.sum(delta * delta, axis=0) + 0.5
        inverse = 1.0 / (dist_sq * jnp.sqrt(dist_sq))
        weight = other[3][:, :, None, :] * inverse
        force = force + jnp.sum(weight[None] * delta, axis=-1)
    return slow_coupling * own[3][None] * force


def fast_from_cells(frac, charge, picked):
    delta = frac[:, :, None] - picked[0:3]
    dist_sq = jnp.sum(delta * delta, axis=0) + 0.5
    inverse = 1.0 / (dist_sq * jnp.sqrt(dist_sq))
    weight = picked[3] * inverse
    return slow_coupling * charge[None, :] * jnp.sum(weight[None] * delta, axis=-1)


def per_device(
    fast_pos,
    fast_vel,
    fast_charge,
    fast_owner,
    exclusions,
    slow_pos,
    slow_vel,
    slow_charge,
    neighbours,
):
    row_count = lax.axis_size("row")
    col_count = lax.axis_size("col")
    row_index = lax.axis_index("row")
    col_index = lax.axis_index("col")
    flat_index = row_index * col_count + col_index
    piece = fast_pos.shape[1]
    cell_rows = slow_pos.shape[1]
    cell_cols = slow_pos.shape[2]
    total_cols = cell_cols * col_count
    coords = owner_coords(fast_owner, total_cols)
    block_width = col_count * piece
    block_start = row_index * block_width
    rows_cells = lax.dynamic_slice_in_dim(coords, block_start, block_width, 1)
    rows_charge = lax.dynamic_slice_in_dim(fast_charge, block_start, block_width, 0)
    rows_exclude = lax.dynamic_slice_in_dim(exclusions, block_start, block_width, 0)
    column_atoms = (
        (jnp.arange(row_count, dtype=jnp.int32) * col_count + col_index)[:, None] * piece
        + jnp.arange(piece, dtype=jnp.int32)[None, :]
    ).reshape(-1)
    column_cells = jnp.take(coords, column_atoms, axis=1)
    column_charge = jnp.take(fast_charge, column_atoms, axis=0)

    def fast_force(frac):
        rows_pos = lax.all_gather(frac, "col", axis=1, tiled=True)
        cols_pos = lax.all_gather(frac, "row", axis=1, tiled=True)
        partial_force = pair_fast(
            rows_pos,
            rows_cells,
            rows_charge,
            rows_exclude,
            cols_pos,
            column_cells,
            column_charge,
            column_atoms,
        )
        return lax.psum_scatter(partial_force, "col", scatter_dimension=1, tiled=True)

    grid_row = fast_owner // total_cols - row_index * cell_rows
    grid_col = fast_owner % total_cols - col_index * cell_cols
    inside = (grid_row >= 0) & (grid_row < cell_rows) & (grid_col >= 0) & (grid_col < cell_cols)
    local_cell = grid_row * cell_cols + grid_col
    cell_ids = jnp.arange(cell_rows * cell_cols, dtype=jnp.int32)
    select = jnp.where(
        inside[:, None] & (local_cell[:, None] == cell_ids[None, :]),
        jnp.float32(1.0),
        jnp.float32(0.0),
    )

    def slow_both(spos, frac):
        data = jnp.concatenate([spos, slow_charge[None]], axis=0)
        padded = with_halo(data, (("row", 1), ("col", 2)), 2)
        views = jnp.stack(
            [padded[:, o // 5 : o // 5 + cell_rows, o % 5 : o % 5 + cell_cols] for o in range(25)]
        )
        cell_force = slow_cells(data, views, neighbours)
        everyone = lax.all_gather(frac, ("row", "col"), axis=1, tiled=True)
        table = jnp.transpose(data, (1, 2, 0, 3)).reshape(cell_rows * cell_cols, 4 * CELL)
        picked = jnp.dot(
            select, table, precision=lax.Precision.HIGHEST, preferred_element_type=jnp.float32
        )
        picked = jnp.transpose(picked.reshape(FAST, 4, CELL), (1, 0, 2))
        partial_env = fast_from_cells(everyone, fast_charge, picked)
        summed = lax.psum(partial_env, ("row", "col"))
        own_env = lax.dynamic_slice_in_dim(summed, flat_index * piece, piece, 1)
        return (cell_force, own_env)

    half_outer = 0.5 * outer_dt
    inner_dt = outer_dt / INNER
    fast_acc = fast_force(fast_pos)
    slow_acc, env_acc = slow_both(slow_pos, fast_pos)
    slow_vel = slow_vel + half_outer * slow_acc
    fast_vel = fast_vel + half_outer * env_acc
    for inner_step in range(INNER):
        fast_vel = fast_vel + 0.5 * inner_dt * fast_acc
        fast_pos = fast_pos + inner_dt * fast_vel
        fast_acc = fast_force(fast_pos)
        fast_vel = fast_vel + 0.5 * inner_dt * fast_acc
    slow_pos = slow_pos + outer_dt * slow_vel
    slow_acc, env_acc = slow_both(slow_pos, fast_pos)
    slow_vel = slow_vel + half_outer * slow_acc
    fast_vel = fast_vel + half_outer * env_acc
    return (fast_pos, fast_vel, slow_pos, slow_vel)


def solution(mesh):
    return jax.shard_map(
        per_device,
        mesh=mesh,
        in_specs=(
            P(None, ("row", "col")),
            P(None, ("row", "col")),
            P(),
            P(),
            P(),
            P(None, "row", "col", None),
            P(None, "row", "col", None),
            P("row", "col", None),
            P("row", "col", None),
        ),
        out_specs=(
            P(None, ("row", "col")),
            P(None, ("row", "col")),
            P(None, "row", "col", None),
            P(None, "row", "col", None),
        ),
        check_vma=False,
    )
```

profile of v0, /device:TPU:0, one launch (start us, length us, event | category | flops | bytes accessed | tf_op | source)
XLA Modules:
  0.0 525.7 jit_solution(1581385438300912036)
XLA Ops:
  11.6 9.6 %all_gather.38 = f32[3,1024]{1,0:T(4,128)S(1)} all-gather(f32[3,128]{1,0:T(4,128)} %param.9), channel_id=1, replica_groups=mesh['row'=8,'col'=4] {'row'}, dimensions={1}, use_global_device_ids=true | all-gather | bytes 13824 | tf_op jit(solution)/shard_map/all_gather | solution.py:103
  21.2 12.3 %all_gather.37 = f32[3,512]{1,0:T(4,128)S(1)} all-gather(f32[3,128]{1,0:T(4,128)} %param.9), channel_id=1, replica_groups=mesh['row'=8,'col'=4] {'col'}, dimensions={1}, use_global_device_ids=true | all-gather | bytes 7680 | tf_op jit(solution)/shard_map/all_gather | solution.py:102
  35.2 6.1 %gather_fusion = f32[1024]{0:T(1024)S(1)} fusion(f32[4096]{0:T(1024)S(1)} %copy-done.2, s32[1024]{0:T(1024)S(1)} %broadcast_clamp_fusion), kind=kCustom, calls=%fused_computation | custom fusion | bytes 12288 | tf_op jit(solution)/shard_map/jit(_take)/gather | solution.py:99
  51.6 65.5 %all_gather.36 = f32[3,4096]{1,0:T(4,128)S(1)} all-gather(f32[3,128]{1,0:T(4,128)S(1)} %copy-done.7), channel_id=1, replica_groups=mesh['row'=8,'col'=4] {'row','col'}, dimensions={1}, use_global_device_ids=true | all-gather | bytes 50688 | tf_op jit(solution)/shard_map/all_gather | solution.py:134
  117.2 6.8 %convolution_bitcast_fusion.1 = f32[4,4096,128]{1,2,0:T(8,128)S(1)} fusion(s32[4096]{0:T(1024)S(1)} %get-tuple-element.54, pred[4096]{0:T(1024)(128)(4,1)S(1)} %compare_and_fusion, f32[1,4,8,128]{3,2,0,1:T(8,128)S(1)} %bitcast.458, f32[3,4,8,128]{3,2,1,0:T(8,128)S(1)} %copy-done.3), kind=kOutput, calls=%fused_computation.29 | convolution fusion | flops 805715968 | bytes 8474624 | tf_op jit(solution)/shard_map/dot_general | solution.py:136
  126.9 38.7 %psum.14 = f32[3,4096]{1,0:T(4,128)S(1)} all-reduce(f32[3,4096]{1,0:T(4,128)S(1)} %broadcast_multiply_fusion.1), channel_id=1, replica_groups=mesh['row'=8,'col'=4] {'row','col'}, use_global_device_ids=true, to_apply=%region_2.3 | all-reduce | flops 12288 | bytes 98304 | tf_op jit(solution)/shard_map/psum | solution.py:141
  166.5 9.7 %all_gather.40 = f32[3,1024]{1,0:T(4,128)S(1)} all-gather(f32[3,128]{1,0:T(4,128)S(1)} %get-tuple-element.36), channel_id=1, replica_groups=mesh['row'=8,'col'=4] {'row'}, dimensions={1}, use_global_device_ids=true | all-gather | bytes 13824 | tf_op jit(solution)/shard_map/all_gather | solution.py:103
  176.2 12.1 %all_gather.39 = f32[3,512]{1,0:T(4,128)S(1)} all-gather(f32[3,128]{1,0:T(4,128)S(1)} %get-tuple-element.36), channel_id=1, replica_groups=mesh['row'=8,'col'=4] {'col'}, dimensions={1}, use_global_device_ids=true | all-gather | bytes 7680 | tf_op jit(solution)/shard_map/all_gather | solution.py:102
  193.7 17.6 %reduce-scatter.18.cloned.1.call-done = f32[128,3]{1,0:T(8,128)} async-done(((f32[512,3]{1,0:T(8,128)}), f32[128,3]{1,0:T(8,128)}) %reduce-scatter.18.cloned.1.call-update) | async-done | bytes 1552
  212.3 8.9 %all_gather.42 = f32[3,1024]{1,0:T(4,128)S(1)} all-gather(f32[3,128]{1,0:T(4,128)S(1)} %multiply_add_fusion.7), channel_id=1, replica_groups=mesh['row'=8,'col'=4] {'row'}, dimensions={1}, use_global_device_ids=true | all-gather | bytes 13824 | tf_op jit(solution)/shard_map/all_gather | solution.py:103
  221.2 11.9 %all_gather.41 = f32[3,512]{1,0:T(4,128)S(1)} all-gather(f32[3,128]{1,0:T(4,128)S(1)} %multiply_add_fusion.7), channel_id=1, replica_groups=mesh['row'=8,'col'=4] {'col'}, dimensions={1}, use_global_device_ids=true | all-gather | bytes 7680 | tf_op jit(solution)/shard_map/all_gather | solution.py:102
  242.4 13.8 %reduce-scatter.20.cloned.1.call-done = f32[128,3]{1,0:T(8,128)} async-done(((f32[512,3]{1,0:T(8,128)}), f32[128,3]{1,0:T(8,128)}) %reduce-scatter.20.cloned.1.call-update) | async-done | bytes 1552
  257.1 8.9 %all_gather.44 = f32[3,1024]{1,0:T(4,128)S(1)} all-gather(f32[3,128]{1,0:T(4,128)S(1)} %get-tuple-element.34), channel_id=1, replica_groups=mesh['row'=8,'col'=4] {'row'}, dimensions={1}, use_global_device_ids=true | all-gather | bytes 13824 | tf_op jit(solution)/shard_map/all_gather | solution.py:103
  266.0 11.9 %all_gather.43 = f32[3,512]{1,0:T(4,128)S(1)} all-gather(f32[3,128]{1,0:T(4,128)S(1)} %get-tuple-element.34), channel_id=1, replica_groups=mesh['row'=8,'col'=4] {'col'}, dimensions={1}, use_global_device_ids=true | all-gather | bytes 7680 | tf_op jit(solution)/shard_map/all_gather | solution.py:102
  283.2 17.7 %reduce-scatter.22.cloned.1.call-done = f32[128,3]{1,0:T(8,128)} async-done(((f32[512,3]{1,0:T(8,128)}), f32[128,3]{1,0:T(8,128)}) %reduce-scatter.22.cloned.1.call-update) | async-done | bytes 1552
  301.8 8.9 %all_gather.46 = f32[3,1024]{1,0:T(4,128)S(1)} all-gather(f32[3,128]{1,0:T(4,128)S(1)} %multiply_add_fusion.5), channel_id=1, replica_groups=mesh['row'=8,'col'=4] {'row'}, dimensions={1}, use_global_device_ids=true | all-gather | bytes 13824 | tf_op jit(solution)/shard_map/all_gather | solution.py:103
  310.7 12.3 %all_gather.45 = f32[3,512]{1,0:T(4,128)S(1)} all-gather(f32[3,128]{1,0:T(4,128)S(1)} %multiply_add_fusion.5), channel_id=1, replica_groups=mesh['row'=8,'col'=4] {'col'}, dimensions={1}, use_global_device_ids=true | all-gather | bytes 7680 | tf_op jit(solution)/shard_map/all_gather | solution.py:102
  328.3 63.9 %all_gather.47 = f32[3,4096]{1,0:T(4,128)S(1)} all-gather(f32[3,128]{1,0:T(4,128)S(1)} %multiply_add_fusion.5), channel_id=1, replica_groups=mesh['row'=8,'col'=4] {'row','col'}, dimensions={1}, use_global_device_ids=true | all-gather | bytes 50688 | tf_op jit(solution)/shard_map/all_gather | solution.py:134
  407.5 7.2 %fusion.3 = (f32[3,4,8,128]{3,2,1,0:T(8,128)S(1)}, f32[4,8,128,128]{3,2,1,0:T(8,128)S(1)}, f32[4,8,128,128]{3,2,1,0:T(8,128)S(1)}, f32[4,8,128,128]{3,2,1,0:T(8,128)S(1)}, f32[3,4,8,128]{3,2,1,0:T(8,128)S(1)}) fusion(f32[4,8,128,128]{3,2,1,0:T(8,128)S(1)} %fusion.51, f32[3,4,8,128]{3,2,1,0:T(8,128)S(1)} %slice_add_fusion.8, ...), kind=kLoop, calls=%fused_computation.33 | loop fusion | flops 21995520 | bytes 10878976 | tf_op jit(solution)/shard_map/reduce_sum | solution.py:56
  417.0 8.3 %fusion.5 = (f32[3,4,8,128]{3,2,1,0:T(8,128)S(1)}, f32[3,4,8,128]{3,2,1,0:T(8,128)S(1)}, f32[3,4,8,128]{3,2,1,0:T(8,128)S(1)}) fusion(f32[4,8,128,128]{3,2,1,0:T(8,128)S(1)} %fusion.53, f32[3,4,8,128]{3,2,1,0:T(8,128)S(1)} %slice_add_fusion.7, f32[3,4,8,128]{3,2,1,0:T(8,128)S(1)} %copy-done.3, f32[3,4,8,128]{3,2,1,0:T(8,128)S(1)} %slice_add_fusion.5, ...), kind=kLoop, calls=%fused_computation.35 | loop fusion | flops 14118912 | bytes 6635520 | tf_op jit(solution)/shard_map/reduce_sum | solution.py:56
  425.4 6.8 %convolution_bitcast_fusion = f32[4,4096,128]{1,2,0:T(8,128)S(1)} fusion(s32[4096]{0:T(1024)S(1)} %get-tuple-element.54, pred[4096]{0:T(1024)(128)(4,1)S(1)} %compare_and_fusion, f32[1,4,8,128]{3,2,1,0:T(8,128)S(1)} %bitcast.464, f32[3,4,8,128]{3,2,1,0:T(8,128)S(1)} %get-tuple-element.32), kind=kOutput, calls=%fused_computation.28 | convolution fusion | flops 805715968 | bytes 8474624 | tf_op jit(solution)/shard_map/dot_general | solution.py:136
  437.6 40.2 %psum.15 = f32[3,4096]{1,0:T(4,128)S(1)} all-reduce(f32[3,4096]{1,0:T(4,128)S(1)} %broadcast_multiply_fusion), channel_id=1, replica_groups=mesh['row'=8,'col'=4] {'row','col'}, use_global_device_ids=true, to_apply=%region_31.32 | all-reduce | flops 12288 | bytes 98304 | tf_op jit(solution)/shard_map/psum | solution.py:141
  500.7 7.2 %fusion.13 = (f32[3,4,8,128]{3,2,1,0:T(8,128)S(1)}, f32[4,8,128,128]{3,2,1,0:T(8,128)S(1)}, f32[4,8,128,128]{3,2,1,0:T(8,128)S(1)}, f32[4,8,128,128]{3,2,1,0:T(8,128)S(1)}, f32[3,4,8,128]{3,2,1,0:T(8,128)S(1)}) fusion(f32[4,8,128,128]{3,2,1,0:T(8,128)S(1)} %fusion.64, f32[3,4,8,128]{3,2,1,0:T(8,128)S(1)} %slice_add_fusion.3, ...), kind=kLoop, calls=%fused_computation.43 | loop fusion | flops 21995520 | bytes 10878976 | tf_op jit(solution)/shard_map/reduce_sum | solution.py:56
  510.2 8.1 %fusion.15 = (f32[3,4,8,128]{3,2,1,0:T(8,128)S(1)}, f32[3,4,8,128]{3,2,1,0:T(8,128)S(1)}, f32[3,4,8,128]{3,2,1,0:T(8,128)S(1)}) fusion(f32[4,8,128,128]{3,2,1,0:T(8,128)S(1)} %fusion.66, f32[3,4,8,128]{3,2,1,0:T(8,128)S(1)} %slice_add_fusion.2, f32[3,4,8,128]{3,2,1,0:T(8,128)S(1)} %get-tuple-element.32, f32[3,4,8,128]{3,2,1,0:T(8,128)S(1)} %slice_add_fusion, ...), kind=kLoop, calls=%fused_computation.45 | loop fusion | flops 14118912 | bytes 6635520 | tf_op jit(solution)/shard_map/reduce_sum | solution.py:56
  (228 shorter events, 96.0 us)
Async XLA Ops:
  7.2 37.4 %copy-start = (s32[4096,4]{0,1:T(4,128)S(1)}, s32[4096,4]{0,1:T(4,128)}, u32[]{:S(2)}) copy-start(s32[4096,4]{0,1:T(4,128)} %param.13) | copy-start | bytes 196612
  7.2 27.9 %copy-start.2 = (f32[4096]{0:T(1024)S(1)}, f32[4096]{0:T(1024)}, u32[]{:S(2)}) copy-start(f32[4096]{0:T(1024)} %param.11) | copy-start | bytes 49156
  7.2 158.4 %reduce-scatter.16.cloned.1.call-start = ((), (), s32[]{:S(2)}) async-start(), calls=%async_computation.5 | async-start | bytes 327680
  8.0 230.4 %collective-permute-start = (f32[4,2,8,128]{3,2,0,1:T(8,128)S(1)}, f32[4,2,8,128]{3,2,0,1:T(8,128)S(1)}, u32[]{:S(2)}, u32[]{:S(2)}) collective-permute-start(f32[4,2,8,128]{3,2,0,1:T(8,128)S(1)} %get-tuple-element.52), channel_id=1, source_target_pairs={{0,4},{4,8},{8,12},{12,16},{16,20},{20,24},{24,28},{28,0},{1,5},{5... | collective-permute-start | bytes 98312 | tf_op jit(solution)/shard_map/ppermute | solution.py:21
  8.5 229.9 %collective-permute-start.1 = (f32[4,2,8,128]{3,2,0,1:T(8,128)S(1)}, f32[4,2,8,128]{3,2,0,1:T(8,128)S(1)}, u32[]{:S(2)}, u32[]{:S(2)}) collective-permute-start(f32[4,2,8,128]{3,2,0,1:T(8,128)S(1)} %get-tuple-element.53), channel_id=1, source_target_pairs={{4,0},{8,4},{12,8},{16,12},{20,16},{24,20},{28,24},{0,28},{5,1},{9... | collective-permute-start | bytes 98312 | tf_op jit(solution)/shard_map/ppermute | solution.py:22
  49.0 2.5 copy-start.5
  49.0 2.6 copy-start.6
  49.0 2.6 copy-start.7
  49.0 68.1 %copy-start.3 = (f32[3,4,8,128]{3,2,1,0:T(8,128)S(1)}, f32[3,4,8,128]{3,2,1,0:T(8,128)}, u32[]{:S(2)}) copy-start(f32[3,4,8,128]{3,2,1,0:T(8,128)} %param.14) | copy-start | bytes 147460
  51.4 160.0 %reduce-scatter.18.cloned.1.call-start = ((), (), s32[]{:S(2)}) async-start(), calls=%async_computation.6 | async-start | bytes 327680
  125.6 40.9 %copy-start.11 = (f32[3,128]{1,0:T(4,128)S(1)}, f32[3,128]{1,0:T(4,128)}, u32[]{:S(2)}) copy-start(f32[3,128]{1,0:T(4,128)} %param.10) | copy-start | bytes 4612
  193.6 62.5 %reduce-scatter.20.cloned.1.call-start = ((), (), s32[]{:S(2)}) async-start(), calls=%async_computation.7 | async-start | bytes 327680
  238.4 62.5 %reduce-scatter.22.cloned.1.call-start = ((), (), s32[]{:S(2)}) async-start(), calls=%async_computation.8 | async-start | bytes 327680
  238.5 154.7 %collective-permute-start.2 = (f32[4,8,2,128]{3,2,0,1:T(2,128)S(1)}, f32[4,8,2,128]{3,2,0,1:T(2,128)S(1)}, u32[]{:S(2)}, u32[]{:S(2)}) collective-permute-start(f32[4,8,2,128]{3,2,0,1:T(2,128)S(1)} %get-tuple-element.45), channel_id=1, source_target_pairs={{0,1},{1,2},{2,3},{3,0},{4,5},{5,6},{6,7},{7,4},{8,9},{9,10},{10,1... | collective-permute-start | bytes 98312 | tf_op jit(solution)/shard_map/ppermute | solution.py:21
  238.5 154.6 %collective-permute-start.3 = (f32[4,8,2,128]{3,2,0,1:T(2,128)S(1)}, f32[4,8,2,128]{3,2,0,1:T(2,128)S(1)}, u32[]{:S(2)}, u32[]{:S(2)}) collective-permute-start(f32[4,8,2,128]{3,2,0,1:T(2,128)S(1)} %get-tuple-element.44), channel_id=1, source_target_pairs={{1,0},{2,1},{3,2},{0,3},{5,4},{6,5},{7,6},{4,7},{9,8},{10,9},{11,1... | collective-permute-start | bytes 98312 | tf_op jit(solution)/shard_map/ppermute | solution.py:22
  283.2 109.1 %reduce-scatter.24.cloned.1.call-start = ((), (), s32[]{:S(2)}) async-start(), calls=%async_computation.9 | async-start | bytes 327680
  301.8 26.5 %copy-start.10 = (f32[3,128]{1,0:T(4,128)}, f32[3,128]{1,0:T(4,128)S(1)}, u32[]{:S(2)}) copy-start(f32[3,128]{1,0:T(4,128)S(1)} %multiply_add_fusion.5) | copy-start | bytes 4612
  417.0 8.3 %copy-start.8 = (f32[3,4,8,128]{3,2,1,0:T(8,128)S(1)}, f32[3,4,8,128]{3,2,1,0:T(8,128)}, u32[]{:S(2)}) copy-start(f32[3,4,8,128]{3,2,1,0:T(8,128)} %param.15) | copy-start | bytes 147460
  425.3 84.9 %copy-start.4 = (f32[3,4,8,128]{3,2,1,0:T(8,128)}, f32[3,4,8,128]{3,2,1,0:T(8,128)S(1)}, u32[]{:S(2)}) copy-start(f32[3,4,8,128]{3,2,1,0:T(8,128)S(1)} %get-tuple-element.32) | copy-start | bytes 147460
  432.2 46.2 %collective-permute-start.4 = (f32[4,2,8,128]{3,2,1,0:T(8,128)S(1)}, f32[4,2,8,128]{3,2,1,0:T(8,128)S(1)}, u32[]{:S(2)}, u32[]{:S(2)}) collective-permute-start(f32[4,2,8,128]{3,2,1,0:T(8,128)S(1)} %get-tuple-element.48), channel_id=1, source_target_pairs={{0,4},{4,8},{8,12},{12,16},{16,20},{20,24},{24,28},{28,0},{1,5},{5... | collective-permute-start | bytes 98312 | tf_op jit(solution)/shard_map/ppermute | solution.py:21
  432.2 46.1 %collective-permute-start.5 = (f32[4,2,8,128]{3,2,1,0:T(8,128)S(1)}, f32[4,2,8,128]{3,2,1,0:T(8,128)S(1)}, u32[]{:S(2)}, u32[]{:S(2)}) collective-permute-start(f32[4,2,8,128]{3,2,1,0:T(8,128)S(1)} %get-tuple-element.49), channel_id=1, source_target_pairs={{4,0},{8,4},{12,8},{16,12},{20,16},{24,20},{28,24},{0,28},{5,1},{9... | collective-permute-start | bytes 98312 | tf_op jit(solution)/shard_map/ppermute | solution.py:22
  478.4 5.8 %collective-permute-start.6 = (f32[4,8,2,128]{3,2,1,0:T(2,128)S(1)}, f32[4,8,2,128]{3,2,1,0:T(2,128)S(1)}, u32[]{:S(2)}, u32[]{:S(2)}) collective-permute-start(f32[4,8,2,128]{3,2,1,0:T(2,128)S(1)} %get-tuple-element.41), channel_id=1, source_target_pairs={{0,1},{1,2},{2,3},{3,0},{4,5},{5,6},{6,7},{7,4},{8,9},{9,10},{10,1... | collective-permute-start | bytes 98312 | tf_op jit(solution)/shard_map/ppermute | solution.py:21
  478.4 5.8 %collective-permute-start.7 = (f32[4,8,2,128]{3,2,1,0:T(2,128)S(1)}, f32[4,8,2,128]{3,2,1,0:T(2,128)S(1)}, u32[]{:S(2)}, u32[]{:S(2)}) collective-permute-start(f32[4,8,2,128]{3,2,1,0:T(2,128)S(1)} %get-tuple-element.40), channel_id=1, source_target_pairs={{1,0},{2,1},{3,2},{0,3},{5,4},{6,5},{7,6},{4,7},{9,8},{10,9},{11,1... | collective-permute-start | bytes 98312 | tf_op jit(solution)/shard_map/ppermute | solution.py:22
  509.4 9.5 %copy-start.1 = (s32[4096,4]{0,1:T(4,128)S(1)}, s32[4096,4]{0,1:T(4,128)}, u32[]{:S(2)}) copy-start(s32[4096,4]{0,1:T(4,128)} %param.13) | copy-start | bytes 196612
  (1 other events, 2.5 us)
Sparse Core Ops, SparseCore 0:
  51.5 18.8 reduce-scatter.15
  193.7 17.5 reduce-scatter.17
  238.5 17.6 reduce-scatter.19
  283.3 17.5 reduce-scatter.21
  328.4 17.6 reduce-scatter.23
where the time goes:
time: 531 us; the launch traced here: 526 us
  blocking collectives  315 us (59%)
  other arithmetic  76.8 us (14%)
  waiting for transfers between devices  50.8 us (10%)
  matrix products  34.2 us (6%)
  local copies, waits for them, and re-layouts  19.3 us (4%)
  between operations  15.2 us (3%)
  starting transfers between devices  14.4 us (3%)
    all_gather x2, blocking collectives, slow_both(): everyone = lax.all_gather(frac, ('row', 'col'), axis=1, tiled=True)  129 us
    psum x2, blocking collectives, slow_both(): summed = lax.psum(partial_env, ('row', 'col'))  78.8 us
    all_gather x5, blocking collectives, fast_force(): rows_pos = lax.all_gather(frac, 'col', axis=1, tiled=True)  60.6 us
    unnamed x10, waiting for transfers between devices  49.2 us
    all_gather x5, blocking collectives, fast_force(): cols_pos = lax.all_gather(frac, 'row', axis=1, tiled=True)  45.9 us
    reduce_sum x4, other arithmetic, slow_cells(): force = force + jnp.sum(weight[None] * delta, axis=-1)  30.7 us
    dot_general x10, matrix products, slow_cells(): jnp.einsum('abo,oxabn->xabn', pick, views, precision=lax.Precision.HIGHEST)  20.6 us
    dot_general x2, matrix products, slow_both(): jnp.dot(select, table, precision=lax.Precision.HIGHEST, preferred_element...  13.6 us
  transfers between devices with their start and end apart: 13, of which 5 were waited for; matrix products, arithmetic and copies ran while one was open for 11% of the time, Pallas kernels for 0%

commit v1 on v0

--- a/solution.py
+++ b/solution.py
@@ -131,7 +131,12 @@
             [padded[:, o // 5 : o // 5 + cell_rows, o % 5 : o % 5 + cell_cols] for o in range(25)]
         )
         cell_force = slow_cells(data, views, neighbours)
-        everyone = lax.all_gather(frac, ("row", "col"), axis=1, tiled=True)
+        everyone = jnp.concatenate(
+            lax.all_to_all(
+                jnp.stack(lax.axis_size(("row", "col")) * [frac], 0), ("row", "col"), 0, 0
+            ),
+            1,
+        )
         table = jnp.transpose(data, (1, 2, 0, 3)).reshape(cell_rows * cell_cols, 4 * CELL)
         picked = jnp.dot(
             select, table, precision=lax.Precision.HIGHEST, preferred_element_type=jnp.float32

time: 531 us -> 434 us (0.82)
  blocking collectives: 315 us -> 185 us
  other arithmetic: 76.8 us -> 91.5 us
  starting transfers between devices: 14.4 us -> 21.2 us
    all_gather x2 -> x0, blocking collectives: 129 us -> none  [slow_both(): everyone = lax.all_gather(frac, ('row', 'col'), axis=1, tiled=True)]
    all_to_all x0 -> x2, starting transfers between devices: none -> 6.16 us  [slow_both(): lax.all_to_all(jnp.stack(lax.axis_size(('row', 'col')) * [frac], 0), ('ro...]
    reduce_sum x2, other arithmetic: 1.69 us -> 7.73 us  [fast_from_cells(): dist_sq = jnp.sum(delta * delta, axis=0) + 0.5]
    reduce_sum x2, other arithmetic: 2.11 us -> 7.75 us  [fast_from_cells(): jnp.sum(weight[None] * delta, axis=-1)]
  transfers between devices with their start and end apart: 13 -> 15, of which waited for: 5 -> 6; matrix products, arithmetic and copies ran while one was open for 11% -> 31% of each run, Pallas kernels for 0% -> 0%
where the time goes in v1:
time: 434 us; the launch traced here: 426 us
  blocking collectives  185 us (43%)
  other arithmetic  91.5 us (21%)
  waiting for transfers between devices  53.9 us (12%)
  matrix products  38.5 us (9%)
  starting transfers between devices  21.2 us (5%)
  local copies, waits for them, and re-layouts  20.7 us (5%)
  between operations  15.5 us (4%)
    psum x2, blocking collectives, slow_both(): summed = lax.psum(partial_env, ('row', 'col'))  78.5 us
    all_gather x5, blocking collectives, fast_force(): rows_pos = lax.all_gather(frac, 'col', axis=1, tiled=True)  60.6 us
    unnamed x10, waiting for transfers between devices  52.3 us
    all_gather x5, blocking collectives, fast_force(): cols_pos = lax.all_gather(frac, 'row', axis=1, tiled=True)  46 us
    reduce_sum x4, other arithmetic, slow_cells(): force = force + jnp.sum(weight[None] * delta, axis=-1)  30.5 us
    dot_general x10, matrix products, slow_cells(): jnp.einsum('abo,oxabn->xabn', pick, views, precision=lax.Precision.HIGHEST)  20.6 us
    dot_general x2, matrix products, slow_both(): jnp.dot(select, table, precision=lax.Precision.HIGHEST, preferred_element...  17.9 us
    ppermute x4, starting transfers between devices, with_halo(): after = lax.ppermute(initial, axis, down)  14 us
  transfers between devices with their start and end apart: 15, of which 6 were waited for; matrix products, arithmetic and copies ran while one was open for 31% of the time, Pallas kernels for 0%

profile of v1, /device:TPU:0, one launch (start us, length us, event | category | flops | bytes accessed | tf_op | source)
XLA Modules:
  0.0 426.2 jit_solution(2174839411865131301)
XLA Ops:
  11.6 9.6 %all_gather.31 = f32[3,1024]{1,0:T(4,128)S(1)} all-gather(f32[3,128]{1,0:T(4,128)} %param.9), channel_id=1, replica_groups=mesh['row'=8,'col'=4] {'row'}, dimensions={1}, use_global_device_ids=true | all-gather | bytes 13824 | tf_op jit(solution)/shard_map/all_gather | solution.py:103
  21.2 12.3 %all_gather.30 = f32[3,512]{1,0:T(4,128)S(1)} all-gather(f32[3,128]{1,0:T(4,128)} %param.9), channel_id=1, replica_groups=mesh['row'=8,'col'=4] {'col'}, dimensions={1}, use_global_device_ids=true | all-gather | bytes 7680 | tf_op jit(solution)/shard_map/all_gather | solution.py:102
  35.2 6.1 %gather_fusion = f32[1024]{0:T(1024)S(1)} fusion(f32[4096]{0:T(1024)S(1)} %copy-done.2, s32[1024]{0:T(1024)S(1)} %broadcast_clamp_fusion), kind=kCustom, calls=%fused_computation | custom fusion | bytes 12288 | tf_op jit(solution)/shard_map/jit(_take)/gather | solution.py:99
  55.8 8.9 %convolution_bitcast_fusion.1 = f32[4,4096,128]{1,2,0:T(8,128)} fusion(s32[4096]{0:T(1024)S(1)} %get-tuple-element.54, pred[4096]{0:T(1024)(128)(4,1)S(1)} %compare_and_fusion, f32[1,4,8,128]{3,2,0,1:T(8,128)S(1)} %bitcast.464, f32[3,4,8,128]{3,2,1,0:T(8,128)S(1)} %copy-done.3), kind=kOutput, calls=%fused_computation.29 | convolution fusion | flops 805715968 | bytes 8474624 | tf_op jit(solution)/shard_map/dot_general | solution.py:141
  64.8 6.4 %reduce-scatter.16.cloned.1.call-done = f32[128,3]{1,0:T(8,128)} async-done(((f32[512,3]{1,0:T(8,128)}), f32[128,3]{1,0:T(8,128)}) %reduce-scatter.16.cloned.1.call-update) | async-done | bytes 1552
  72.2 4.3 %collective-permute-start.3 = (f32[4,8,2,128]{3,2,0,1:T(2,128)S(1)}, f32[4,8,2,128]{3,2,0,1:T(2,128)S(1)}, u32[]{:S(2)}, u32[]{:S(2)}) collective-permute-start(f32[4,8,2,128]{3,2,0,1:T(2,128)S(1)} %get-tuple-element.44), channel_id=1, source_target_pairs={{1,0},{2,1},{3,2},{0,3},{5,4},{6,5},{7,6},{4,7},{9,8},{10,9},{11,1... | collective-permute-start | bytes 98312 | tf_op jit(solution)/shard_map/ppermute | solution.py:22
  92.4 7.2 %fusion.3 = (f32[3,4,8,128]{3,2,1,0:T(8,128)S(1)}, f32[4,8,128,128]{3,2,1,0:T(8,128)S(1)}, f32[4,8,128,128]{3,2,1,0:T(8,128)S(1)}, f32[4,8,128,128]{3,2,1,0:T(8,128)S(1)}, f32[3,4,8,128]{3,2,1,0:T(8,128)S(1)}) fusion(f32[4,8,128,128]{3,2,1,0:T(8,128)S(1)} %fusion.51, f32[3,4,8,128]{3,2,1,0:T(8,128)S(1)} %slice_add_fusion.8, ...), kind=kLoop, calls=%fused_computation.33 | loop fusion | flops 21995520 | bytes 10878976 | tf_op jit(solution)/shard_map/reduce_sum | solution.py:56
  101.9 8.1 %fusion.5 = (f32[3,4,8,128]{3,2,1,0:T(8,128)S(1)}, f32[3,4,8,128]{3,2,1,0:T(8,128)S(1)}, f32[3,4,8,128]{3,2,1,0:T(8,128)S(1)}) fusion(f32[4,8,128,128]{3,2,1,0:T(8,128)S(1)} %fusion.53, f32[3,4,8,128]{3,2,1,0:T(8,128)S(1)} %slice_add_fusion.7, f32[3,4,8,128]{3,2,1,0:T(8,128)S(1)} %copy-done.3, f32[3,4,8,128]{3,2,1,0:T(8,128)S(1)} %slice_add_fusion.5, ...), kind=kLoop, calls=%fused_computation.35 | loop fusion | flops 14118912 | bytes 6635520 | tf_op jit(solution)/shard_map/reduce_sum | solution.py:56
  110.0 9.0 %convolution_bitcast_fusion = f32[4,4096,128]{1,2,0:T(8,128)} fusion(s32[4096]{0:T(1024)S(1)} %get-tuple-element.54, pred[4096]{0:T(1024)(128)(4,1)S(1)} %compare_and_fusion, f32[1,4,8,128]{3,2,1,0:T(8,128)S(1)} %bitcast.469, f32[3,4,8,128]{3,2,1,0:T(8,128)S(1)} %get-tuple-element.32), kind=kOutput, calls=%fused_computation.28 | convolution fusion | flops 805715968 | bytes 8474624 | tf_op jit(solution)/shard_map/dot_general | solution.py:141
  132.2 39.7 %psum.14 = f32[3,4096]{1,0:T(4,128)S(1)} all-reduce(f32[3,4096]{1,0:T(4,128)S(1)} %broadcast_multiply_fusion.1), channel_id=1, replica_groups=mesh['row'=8,'col'=4] {'row','col'}, use_global_device_ids=true, to_apply=%region_2.3 | all-reduce | flops 12288 | bytes 98304 | tf_op jit(solution)/shard_map/psum | solution.py:146
  172.0 9.7 %all_gather.33 = f32[3,1024]{1,0:T(4,128)S(1)} all-gather(f32[3,128]{1,0:T(4,128)S(1)} %get-tuple-element.36), channel_id=1, replica_groups=mesh['row'=8,'col'=4] {'row'}, dimensions={1}, use_global_device_ids=true | all-gather | bytes 13824 | tf_op jit(solution)/shard_map/all_gather | solution.py:103
  181.6 12.5 %all_gather.32 = f32[3,512]{1,0:T(4,128)S(1)} all-gather(f32[3,128]{1,0:T(4,128)S(1)} %get-tuple-element.36), channel_id=1, replica_groups=mesh['row'=8,'col'=4] {'col'}, dimensions={1}, use_global_device_ids=true | all-gather | bytes 7680 | tf_op jit(solution)/shard_map/all_gather | solution.py:102
  203.4 13.8 %reduce-scatter.18.cloned.1.call-done = f32[128,3]{1,0:T(8,128)} async-done(((f32[512,3]{1,0:T(8,128)}), f32[128,3]{1,0:T(8,128)}) %reduce-scatter.18.cloned.1.call-update) | async-done | bytes 1552
  218.1 8.9 %all_gather.35 = f32[3,1024]{1,0:T(4,128)S(1)} all-gather(f32[3,128]{1,0:T(4,128)S(1)} %multiply_add_fusion.7), channel_id=1, replica_groups=mesh['row'=8,'col'=4] {'row'}, dimensions={1}, use_global_device_ids=true | all-gather | bytes 13824 | tf_op jit(solution)/shard_map/all_gather | solution.py:103
  227.0 11.9 %all_gather.34 = f32[3,512]{1,0:T(4,128)S(1)} all-gather(f32[3,128]{1,0:T(4,128)S(1)} %multiply_add_fusion.7), channel_id=1, replica_groups=mesh['row'=8,'col'=4] {'col'}, dimensions={1}, use_global_device_ids=true | all-gather | bytes 7680 | tf_op jit(solution)/shard_map/all_gather | solution.py:102
  244.3 17.7 %reduce-scatter.20.cloned.1.call-done = f32[128,3]{1,0:T(8,128)} async-done(((f32[512,3]{1,0:T(8,128)}), f32[128,3]{1,0:T(8,128)}) %reduce-scatter.20.cloned.1.call-update) | async-done | bytes 1552
  262.9 8.9 %all_gather.37 = f32[3,1024]{1,0:T(4,128)S(1)} all-gather(f32[3,128]{1,0:T(4,128)S(1)} %get-tuple-element.34), channel_id=1, replica_groups=mesh['row'=8,'col'=4] {'row'}, dimensions={1}, use_global_device_ids=true | all-gather | bytes 13824 | tf_op jit(solution)/shard_map/all_gather | solution.py:103
  271.8 11.9 %all_gather.36 = f32[3,512]{1,0:T(4,128)S(1)} all-gather(f32[3,128]{1,0:T(4,128)S(1)} %get-tuple-element.34), channel_id=1, replica_groups=mesh['row'=8,'col'=4] {'col'}, dimensions={1}, use_global_device_ids=true | all-gather | bytes 7680 | tf_op jit(solution)/shard_map/all_gather | solution.py:102
  305.7 7.2 %fusion.13 = (f32[3,4,8,128]{3,2,1,0:T(8,128)S(1)}, f32[4,8,128,128]{3,2,1,0:T(8,128)S(1)}, f32[4,8,128,128]{3,2,1,0:T(8,128)S(1)}, f32[4,8,128,128]{3,2,1,0:T(8,128)S(1)}, f32[3,4,8,128]{3,2,1,0:T(8,128)S(1)}) fusion(f32[4,8,128,128]{3,2,1,0:T(8,128)S(1)} %fusion.64, f32[3,4,8,128]{3,2,1,0:T(8,128)S(1)} %slice_add_fusion.3, ...), kind=kLoop, calls=%fused_computation.43 | loop fusion | flops 21995520 | bytes 10878976 | tf_op jit(solution)/shard_map/reduce_sum | solution.py:56
  315.2 8.1 %fusion.15 = (f32[3,4,8,128]{3,2,1,0:T(8,128)S(1)}, f32[3,4,8,128]{3,2,1,0:T(8,128)S(1)}, f32[3,4,8,128]{3,2,1,0:T(8,128)S(1)}) fusion(f32[4,8,128,128]{3,2,1,0:T(8,128)S(1)} %fusion.66, f32[3,4,8,128]{3,2,1,0:T(8,128)S(1)} %slice_add_fusion.2, f32[3,4,8,128]{3,2,1,0:T(8,128)S(1)} %get-tuple-element.32, f32[3,4,8,128]{3,2,1,0:T(8,128)S(1)} %slice_add_fusion, ...), kind=kLoop, calls=%fused_computation.45 | loop fusion | flops 14118912 | bytes 6635520 | tf_op jit(solution)/shard_map/reduce_sum | solution.py:56
  324.3 8.9 %all_gather.39 = f32[3,1024]{1,0:T(4,128)S(1)} all-gather(f32[3,128]{1,0:T(4,128)S(1)} %multiply_add_fusion.5), channel_id=1, replica_groups=mesh['row'=8,'col'=4] {'row'}, dimensions={1}, use_global_device_ids=true | all-gather | bytes 13824 | tf_op jit(solution)/shard_map/all_gather | solution.py:103
  333.1 11.9 %all_gather.38 = f32[3,512]{1,0:T(4,128)S(1)} all-gather(f32[3,128]{1,0:T(4,128)S(1)} %multiply_add_fusion.5), channel_id=1, replica_groups=mesh['row'=8,'col'=4] {'col'}, dimensions={1}, use_global_device_ids=true | all-gather | bytes 7680 | tf_op jit(solution)/shard_map/all_gather | solution.py:102
  354.4 14.4 %reduce-scatter.24.cloned.1.call-done = f32[128,3]{1,0:T(8,128)} async-done(((f32[512,3]{1,0:T(8,128)}), f32[128,3]{1,0:T(8,128)}) %reduce-scatter.24.cloned.1.call-update) | async-done | bytes 1552
  379.9 38.7 %psum.15 = f32[3,4096]{1,0:T(4,128)S(1)} all-reduce(f32[3,4096]{1,0:T(4,128)S(1)} %broadcast_multiply_fusion), channel_id=1, replica_groups=mesh['row'=8,'col'=4] {'row','col'}, use_global_device_ids=true, to_apply=%region_31.32 | all-reduce | flops 12288 | bytes 98304 | tf_op jit(solution)/shard_map/psum | solution.py:146
  (232 shorter events, 114.7 us)
Async XLA Ops:
  7.2 37.4 %copy-start = (s32[4096,4]{0,1:T(4,128)S(1)}, s32[4096,4]{0,1:T(4,128)}, u32[]{:S(2)}) copy-start(s32[4096,4]{0,1:T(4,128)} %param.13) | copy-start | bytes 196612
  7.2 27.9 %copy-start.2 = (f32[4096]{0:T(1024)S(1)}, f32[4096]{0:T(1024)}, u32[]{:S(2)}) copy-start(f32[4096]{0:T(1024)} %param.11) | copy-start | bytes 49156
  7.2 64.0 %reduce-scatter.16.cloned.1.call-start = ((), (), s32[]{:S(2)}) async-start(), calls=%async_computation.7 | async-start | bytes 327680
  8.0 64.0 %collective-permute-start = (f32[4,2,8,128]{3,2,0,1:T(8,128)S(1)}, f32[4,2,8,128]{3,2,0,1:T(8,128)S(1)}, u32[]{:S(2)}, u32[]{:S(2)}) collective-permute-start(f32[4,2,8,128]{3,2,0,1:T(8,128)S(1)} %get-tuple-element.52), channel_id=1, source_target_pairs={{0,4},{4,8},{8,12},{12,16},{16,20},{20,24},{24,28},{28,0},{1,5},{5... | collective-permute-start | bytes 98312 | tf_op jit(solution)/shard_map/ppermute | solution.py:21
  8.5 63.5 %collective-permute-start.1 = (f32[4,2,8,128]{3,2,0,1:T(8,128)S(1)}, f32[4,2,8,128]{3,2,0,1:T(8,128)S(1)}, u32[]{:S(2)}, u32[]{:S(2)}) collective-permute-start(f32[4,2,8,128]{3,2,0,1:T(8,128)S(1)} %get-tuple-element.53), channel_id=1, source_target_pairs={{4,0},{8,4},{12,8},{16,12},{20,16},{24,20},{28,24},{0,28},{5,1},{9... | collective-permute-start | bytes 98312 | tf_op jit(solution)/shard_map/ppermute | solution.py:22
  49.0 6.5 %copy-start.6 = (s32[4096]{0:T(1024)S(1)}, s32[4096]{0:T(1024)}, u32[]{:S(2)}) copy-start(s32[4096]{0:T(1024)} %param.12) | copy-start | bytes 49156
  49.0 6.7 %copy-start.3 = (f32[3,4,8,128]{3,2,1,0:T(8,128)S(1)}, f32[3,4,8,128]{3,2,1,0:T(8,128)}, u32[]{:S(2)}) copy-start(f32[3,4,8,128]{3,2,1,0:T(8,128)} %param.14) | copy-start | bytes 147460
  52.1 70.0 %all-to-all-start = ((f32[32,3,128]{2,1,0:T(4,128)}), f32[32,3,128]{2,1,0:T(4,128)S(1)}, u32[]{:S(2)}, u32[]{:S(2)}) async-start(f32[32,3,128]{2,1,0:T(4,128)} %stack.124), calls=%async_computation | async-start | bytes 131072 | tf_op jit(solution)/shard_map/all_to_all | solution.py:135
  55.4 161.8 %reduce-scatter.18.cloned.1.call-start = ((), (), s32[]{:S(2)}) async-start(), calls=%async_computation.8 | async-start | bytes 327680
  72.1 5.8 %collective-permute-start.2 = (f32[4,8,2,128]{3,2,0,1:T(2,128)S(1)}, f32[4,8,2,128]{3,2,0,1:T(2,128)S(1)}, u32[]{:S(2)}, u32[]{:S(2)}) collective-permute-start(f32[4,8,2,128]{3,2,0,1:T(2,128)S(1)} %get-tuple-element.45), channel_id=1, source_target_pairs={{0,1},{1,2},{2,3},{3,0},{4,5},{5,6},{6,7},{7,4},{8,9},{9,10},{10,1... | collective-permute-start | bytes 98312 | tf_op jit(solution)/shard_map/ppermute | solution.py:21
  72.2 5.9 %collective-permute-start.3 = (f32[4,8,2,128]{3,2,0,1:T(2,128)S(1)}, f32[4,8,2,128]{3,2,0,1:T(2,128)S(1)}, u32[]{:S(2)}, u32[]{:S(2)}) collective-permute-start(f32[4,8,2,128]{3,2,0,1:T(2,128)S(1)} %get-tuple-element.44), channel_id=1, source_target_pairs={{1,0},{2,1},{3,2},{0,3},{5,4},{6,5},{7,6},{4,7},{9,8},{10,9},{11,1... | collective-permute-start | bytes 98312 | tf_op jit(solution)/shard_map/ppermute | solution.py:22
  101.9 8.1 %copy-start.8 = (f32[3,4,8,128]{3,2,1,0:T(8,128)S(1)}, f32[3,4,8,128]{3,2,1,0:T(8,128)}, u32[]{:S(2)}) copy-start(f32[3,4,8,128]{3,2,1,0:T(8,128)} %param.15) | copy-start | bytes 147460
  110.0 205.2 %copy-start.4 = (f32[3,4,8,128]{3,2,1,0:T(8,128)}, f32[3,4,8,128]{3,2,1,0:T(8,128)S(1)}, u32[]{:S(2)}) copy-start(f32[3,4,8,128]{3,2,1,0:T(8,128)S(1)} %get-tuple-element.32) | copy-start | bytes 147460
  119.0 80.4 %collective-permute-start.4 = (f32[4,2,8,128]{3,2,1,0:T(8,128)S(1)}, f32[4,2,8,128]{3,2,1,0:T(8,128)S(1)}, u32[]{:S(2)}, u32[]{:S(2)}) collective-permute-start(f32[4,2,8,128]{3,2,1,0:T(8,128)S(1)} %get-tuple-element.48), channel_id=1, source_target_pairs={{0,4},{4,8},{8,12},{12,16},{16,20},{20,24},{24,28},{28,0},{1,5},{5... | collective-permute-start | bytes 98312 | tf_op jit(solution)/shard_map/ppermute | solution.py:21
  119.1 80.4 %collective-permute-start.5 = (f32[4,2,8,128]{3,2,1,0:T(8,128)S(1)}, f32[4,2,8,128]{3,2,1,0:T(8,128)S(1)}, u32[]{:S(2)}, u32[]{:S(2)}) collective-permute-start(f32[4,2,8,128]{3,2,1,0:T(8,128)S(1)} %get-tuple-element.49), channel_id=1, source_target_pairs={{4,0},{8,4},{12,8},{16,12},{20,16},{24,20},{28,24},{0,28},{5,1},{9... | collective-permute-start | bytes 98312 | tf_op jit(solution)/shard_map/ppermute | solution.py:22
  128.3 43.6 %copy-start.11 = (f32[3,128]{1,0:T(4,128)S(1)}, f32[3,128]{1,0:T(4,128)}, u32[]{:S(2)}) copy-start(f32[3,128]{1,0:T(4,128)} %param.10) | copy-start | bytes 4612
  199.4 62.5 %reduce-scatter.20.cloned.1.call-start = ((), (), s32[]{:S(2)}) async-start(), calls=%async_computation.9 | async-start | bytes 327680
  199.5 89.7 %collective-permute-start.6 = (f32[4,8,2,128]{3,2,1,0:T(2,128)S(1)}, f32[4,8,2,128]{3,2,1,0:T(2,128)S(1)}, u32[]{:S(2)}, u32[]{:S(2)}) collective-permute-start(f32[4,8,2,128]{3,2,1,0:T(2,128)S(1)} %get-tuple-element.41), channel_id=1, source_target_pairs={{0,1},{1,2},{2,3},{3,0},{4,5},{5,6},{6,7},{7,4},{8,9},{9,10},{10,1... | collective-permute-start | bytes 98312 | tf_op jit(solution)/shard_map/ppermute | solution.py:21
  199.7 89.5 %collective-permute-start.7 = (f32[4,8,2,128]{3,2,1,0:T(2,128)S(1)}, f32[4,8,2,128]{3,2,1,0:T(2,128)S(1)}, u32[]{:S(2)}, u32[]{:S(2)}) collective-permute-start(f32[4,8,2,128]{3,2,1,0:T(2,128)S(1)} %get-tuple-element.40), channel_id=1, source_target_pairs={{1,0},{2,1},{3,2},{0,3},{5,4},{6,5},{7,6},{4,7},{9,8},{10,9},{11,1... | collective-permute-start | bytes 98312 | tf_op jit(solution)/shard_map/ppermute | solution.py:22
  244.2 79.1 %reduce-scatter.22.cloned.1.call-start = ((), (), s32[]{:S(2)}) async-start(), calls=%async_computation.10 | async-start | bytes 327680
  289.0 79.8 %reduce-scatter.24.cloned.1.call-start = ((), (), s32[]{:S(2)}) async-start(), calls=%async_computation.11 | async-start | bytes 327680
  324.2 26.1 %copy-start.10 = (f32[3,128]{1,0:T(4,128)}, f32[3,128]{1,0:T(4,128)S(1)}, u32[]{:S(2)}) copy-start(f32[3,128]{1,0:T(4,128)S(1)} %multiply_add_fusion.5) | copy-start | bytes 4612
  351.0 18.8 %all-to-all-start.1 = ((f32[32,3,128]{2,1,0:T(4,128)}), f32[32,3,128]{2,1,0:T(4,128)S(1)}, u32[]{:S(2)}, u32[]{:S(2)}) async-start(f32[32,3,128]{2,1,0:T(4,128)} %stack.310), calls=%async_computation.1 | async-start | bytes 131072 | tf_op jit(solution)/shard_map/all_to_all | solution.py:135
  376.0 43.3 %copy-start.1 = (s32[4096,4]{0,1:T(4,128)S(1)}, s32[4096,4]{0,1:T(4,128)}, u32[]{:S(2)}) copy-start(s32[4096,4]{0,1:T(4,128)} %param.13) | copy-start | bytes 196612
  (3 other events, 15.5 us)
Sparse Core Ops, SparseCore 0:
  51.5 19.5 reduce-scatter.15
  199.5 17.5 reduce-scatter.17
  244.3 17.5 reduce-scatter.19
  289.1 17.5 reduce-scatter.21
  350.5 18.3 reduce-scatter.23
